TPU v7x, 32 devices: a whole 2x2x4 slice. The times are simulated.
32 devices in a mesh: groups: 2 (over y), pool: 4 (over x, core), tp: 4 (over z).
Axes of the slice: x: 2, y: 2, z: 4, core: 2. Of those that a mesh axis runs over, the one named last changes fastest.
Arguments:
- queries: bfloat16 [192, 16384], P(('groups', 'pool', 'tp')), parts along dimension 0, may hold values from -6 to 6
- cached_entries: bfloat16 [192, 512, 512], P(('groups', 'pool', 'tp')), parts along dimension 0, may hold values from -4.5 to 4.5
- new_entry: bfloat16 [192, 512], P(('groups', 'pool', 'tp')), parts along dimension 0, may hold values from -4.5 to 4.5
- lengths: int32 [192], P(('groups', 'pool', 'tp')), parts along dimension 0, may hold values from 2 to 512, as said below
- residual: bfloat16 [192, 7168], P(('groups', 'pool'), 'tp'), parts along dimension 0, may hold values from -40 to 40
- out_weight: bfloat16 [16384, 7168], P('pool', 'tp'), may hold values from -0.046875 to 0.046875
- norm_gain: bfloat16 [7168], P('tp'), may hold values from 0.5 to 1.5
- gate_weight: bfloat16 [7168, 18432], P('tp', 'pool'), may hold values from -0.0625 to 0.0625
- up_weight: bfloat16 [7168, 18432], P('tp', 'pool'), may hold values from -0.0625 to 0.0625
- down_weight: bfloat16 [18432, 7168], P('pool', 'tp'), may hold values from -0.046875 to 0.046875
Outputs:
- layer_out: bfloat16 [192, 7168], P(('groups', 'pool'), 'tp'), parts along dimension 0
There are 2 independent parts, one for each index of `groups`. A program takes and returns all parts, laid end to end along the dimension named above; an argument that names none is the same for every part. Nothing has to cross between parts.
Inputs may be any that keep to these rules, and one draw needn't show every extreme that they name: `lengths`: every request has at least 2 positions in use and at most 512; some request of every draw has exactly 512.
All inputs are finite; a program needn't handle non-finite values.
Results may differ from a plain program's by a relative error of at most 0.009.
Values may be sent and summed in bfloat16 or wider, within the bound.
A program may use at most 192 MiB of HBM per device.

v0:
```python
import math
import jax
import jax.numpy as jnp
from jax import lax
from jax.sharding import PartitionSpec as P

D = 7168
HEADS = 64
HD = 256
epsilon = 1e-06


def attend(queries, cached_entries, new_entry, lengths):
    amount = queries.shape[0]
    query_heads = queries.reshape(amount, HEADS, HD)
    key_rows = cached_entries[:, :, :HD]
    value_rows = cached_entries[:, :, HD:]
    factor = 1.0 / math.sqrt(HD)
    scores = (
        jnp.einsum("rhd,rld->rhl", query_heads, key_rows, preferred_element_type=jnp.float32)
        * factor
    )
    own_score = (
        jnp.einsum("rhd,rd->rh", query_heads, new_entry[:, :HD], preferred_element_type=jnp.float32)
        * factor
    )
    positions = lax.broadcasted_iota(jnp.int32, scores.shape, 2)
    usable = positions < lengths[:, None, None]
    scores = jnp.where(usable, scores, -jnp.inf)
    peak_score = jnp.maximum(jnp.max(scores, axis=2), own_score)
    weights_raw = jnp.where(usable, jnp.exp(scores - peak_score[:, :, None]), 0.0)
    own_raw = jnp.exp(own_score - peak_score)
    totals = jnp.sum(weights_raw, axis=2) + own_raw
    weights = (weights_raw / totals[:, :, None]).astype(jnp.bfloat16)
    own_weight = (own_raw / totals).astype(jnp.bfloat16)
    mixture = jnp.einsum("rhl,rld->rhd", weights, value_rows, preferred_element_type=jnp.float32)
    mixture = mixture + own_weight.astype(jnp.float32)[:, :, None] * new_entry[:, None, HD:].astype(
        jnp.float32
    )
    return mixture.reshape(amount, HEADS * HD).astype(jnp.bfloat16)


def finish_rows(
    queries,
    cached_entries,
    new_entry,
    lengths,
    resid_rows,
    out_weight,
    norm_gain,
    gate_weight,
    up_weight,
    down_weight,
):
    shard_count = lax.axis_size("tp")
    pool_at = lax.axis_index("pool")
    attended = attend(queries, cached_entries, new_entry, lengths)
    columns = lax.all_gather(attended, "tp", axis=0, tiled=True)
    spread = lax.all_to_all(columns, "pool", split_axis=1, concat_axis=0, tiled=True)
    block_rows = shard_count * queries.shape[0]
    resid_flat = resid_rows.reshape(block_rows, resid_rows.shape[2]).astype(jnp.float32)
    gain_row = norm_gain.astype(jnp.float32)[None, :]
    partial_value = jnp.dot(spread, out_weight, preferred_element_type=jnp.float32)
    own_rows = (
        lax.dynamic_slice_in_dim(partial_value, pool_at * block_rows, block_rows, 0) + resid_flat
    )
    summand = lax.dynamic_update_slice_in_dim(partial_value, own_rows, pool_at * block_rows, 0)
    post_attn = lax.psum(summand, "pool")
    scaled = (post_attn * gain_row).astype(jnp.bfloat16)
    squares = jnp.sum(post_attn * post_attn, axis=1)
    own_post = lax.dynamic_slice_in_dim(post_attn, pool_at * block_rows, block_rows, 0)
    gate_part = jnp.dot(scaled, gate_weight, preferred_element_type=jnp.float32)
    up_part = jnp.dot(scaled, up_weight, preferred_element_type=jnp.float32)
    gate_sum, up_sum, square_sum = (
        lax.psum(gate_part.astype(jnp.bfloat16), "tp").astype(jnp.float32),
        lax.psum(up_part.astype(jnp.bfloat16), "tp").astype(jnp.float32),
        lax.psum(squares.astype(jnp.bfloat16), "tp").astype(jnp.float32),
    )
    inv_rms = lax.rsqrt(square_sum / D + epsilon)
    hidden = (jax.nn.silu(gate_sum * inv_rms[:, None]) * (up_sum * inv_rms[:, None])).astype(
        jnp.bfloat16
    )
    down_sum = lax.psum_scatter(
        jnp.dot(hidden, down_weight, preferred_element_type=jnp.float32).astype(jnp.bfloat16),
        "pool",
        scatter_dimension=0,
        tiled=True,
    ).astype(jnp.float32)
    return (own_post + down_sum).astype(jnp.bfloat16)


def on_device(
    queries,
    cached_entries,
    new_entry,
    lengths,
    residual,
    out_weight,
    norm_gain,
    gate_weight,
    up_weight,
    down_weight,
):
    shard_count = lax.axis_size("tp")
    amount = queries.shape[0]
    resid_rows = residual.reshape(shard_count, amount, residual.shape[1])
    result = finish_rows(
        queries,
        cached_entries,
        new_entry,
        lengths,
        resid_rows,
        out_weight,
        norm_gain,
        gate_weight,
        up_weight,
        down_weight,
    )
    return result


def solution(mesh):
    placed = (
        P(("groups", "pool", "tp"), None),
        P(("groups", "pool", "tp"), None, None),
        P(("groups", "pool", "tp"), None),
        P(("groups", "pool", "tp")),
        P(("groups", "pool"), "tp"),
        P("pool", "tp"),
        P("tp"),
        P("tp", "pool"),
        P("tp", "pool"),
        P("pool", "tp"),
    )
    return jax.shard_map(
        on_device,
        mesh=mesh,
        in_specs=placed,
        out_specs=P(("groups", "pool"), "tp"),
        check_vma=False,
    )
```

profile of v0, /device:TPU:0, one launch (start us, length us, event | category | flops | bytes accessed | tf_op | source)
XLA Modules:
  0.0 228.4 jit_solution(9095619187333805453)
XLA Ops:
  6.5 0.0 copy-start.5
  6.5 0.0 copy-start.4
  6.5 0.9 slice_convert_fusion
  7.4 1.2 fusion.23
  8.6 2.1 fusion.36
  10.8 0.0 copy-done.4
  10.8 0.3 fusion.18
  11.1 0.0 copy-done.5
  11.1 0.5 fusion.13
  11.6 0.2 reshape.17
  11.8 24.2 %all-gather = bf16[4,6,16384]{2,1,0:T(8,128)(2,1)S(1)} all-gather(bf16[1,6,16384]{2,1,0:T(8,128)(2,1)S(1)} %reshape.17), channel_id=1, replica_groups=mesh['groups'=2,'pool'=4,'tp'=4] {'tp'}, dimensions={0}, use_global_device_ids=true | all-gather | bytes 983040 | tf_op jit(solution)/shard_map/all_gather | solution.py:58
  36.0 1.1 all_to_all.14
  37.1 1.3 copy.12
  38.4 3.5 %all-to-all-start = ((bf16[24,4,4096]{2,0,1:T(8,128)(2,1)}), bf16[24,4,4096]{2,0,1:T(8,128)(2,1)S(1)}, u32[]{:S(2)}, u32[]{:S(2)}) async-start(bf16[24,4,4096]{2,0,1:T(8,128)(2,1)} %copy.12), calls=%async_computation | async-start | bytes 1572864 | tf_op jit(solution)/shard_map/all_to_all | solution.py:59
  41.9 0.0 all-reduce.4.cloned.1.call-start
  42.0 11.6 %all-to-all-done = bf16[24,4,4096]{2,0,1:T(8,128)(2,1)S(1)} async-done(((bf16[24,4,4096]{2,0,1:T(8,128)(2,1)}), bf16[24,4,4096]{2,0,1:T(8,128)(2,1)S(1)}, u32[]{:S(2)}, u32[]{:S(2)}) %all-to-all-start) | async-done | bytes 786464 | tf_op jit(solution)/shard_map/all_to_all | solution.py:59
  53.5 0.0 copy-start.2
  53.5 0.0 copy-start.3
  53.5 7.6 %fusion.37 = f32[96,1792]{1,0:T(8,128)S(1)} fusion(bf16[96,4096]{1,0:T(8,128)(2,1)S(1)} %bitcast.36, bf16[4096,1792]{1,0:T(8,128)(2,1)} %param.15), kind=kOutput, calls=%fused_computation.45 | convolution fusion | flops 1409286144 | bytes 16154624 | tf_op jit(solution)/shard_map/dot_general | solution.py:63
  61.2 0.0 copy-done.2
  61.2 0.0 copy-start.1
  61.2 0.8 copy-done.1
  62.1 0.0 all-reduce.4.cloned.1.call-update
  62.1 0.0 all-reduce.6.cloned.1.call-start
  62.2 0.0 copy-done.3
  62.2 33.4 %all-reduce.4.cloned.1.call-done = f32[96,1792]{1,0:T(8,128)} async-done(((f32[96,1792]{1,0:T(8,128)}), f32[96,1792]{1,0:T(8,128)}) %all-reduce.4.cloned.1.call-update) | async-done | bytes 688144 | tf_op jit(solution)/shard_map/psum | solution.py:68
  95.5 0.0 copy-start
  95.5 9.6 %convolution_convert_fusion = bf16[96,4608]{1,0:T(8,128)(2,1)} fusion(bf16[1792,4608]{1,0:T(8,128)(2,1)} %param.18, f32[96,1792]{1,0:T(8,128)} %all-reduce.4.cloned.1.call-done, f32[1792]{0:T(1024)S(1)} %convert_element_type.65), kind=kOutput, calls=%fused_computation | convolution fusion | flops 1586233344 | bytes 18095104 | tf_op jit(solution)/shard_map/dot_general | solution.py:73
  105.2 0.0 copy-done
  105.2 9.4 %convolution_convert_fusion.1 = bf16[96,4608]{1,0:T(8,128)(2,1)} fusion(bf16[1792,4608]{1,0:T(8,128)(2,1)} %param.17, f32[96,1792]{1,0:T(8,128)S(1)} %copy-done, f32[1792]{0:T(1024)S(1)} %convert_element_type.65), kind=kOutput, calls=%fused_computation.1 | convolution fusion | flops 1586233344 | bytes 18095104 | tf_op jit(solution)/shard_map/dot_general | solution.py:72
  114.5 0.0 all-reduce.6.cloned.1.call-update
  114.5 0.0 reduce-scatter.2.cloned.1.call-start
  114.6 0.1 multiply_reduce_fusion
  114.7 12.2 %psum.30 = bf16[96]{0:T(256)(128)(2,1)S(1)} all-reduce(bf16[96]{0:T(256)(128)(2,1)S(1)} %multiply_reduce_fusion), channel_id=1, replica_groups=mesh['groups'=2,'pool'=4,'tp'=4] {'tp'}, use_global_device_ids=true, to_apply=%region_5.6 | all-reduce | flops 96 | bytes 384 | tf_op jit(solution)/shard_map/psum | solution.py:77
  126.9 63.7 %all-reduce.6.cloned.1.call-done = (bf16[96,4608]{1,0:T(8,128)(2,1)}, bf16[96,4608]{1,0:T(8,128)(2,1)}) async-done(((bf16[96,4608]{1,0:T(8,128)(2,1)}, bf16[96,4608]{1,0:T(8,128)(2,1)}), (bf16[96,4608]{1,0:T(8,128)(2,1)}, bf16[96,4608]{1,0:T(8,128)(2,1)})) %all-reduce.6.cloned.1.call-update) | async-done | bytes 1769488 | tf_op jit(solution)/shard_map/psum | solution.py:76
  190.6 9.9 %convolution_convert_fusion.2 = bf16[96,1792]{1,0:T(8,128)(2,1)} fusion(bf16[4608,1792]{1,0:T(8,128)(2,1)} %param.19, bf16[96,4608]{1,0:T(8,128)(2,1)} %get-tuple-element.5, bf16[96,4608]{1,0:T(8,128)(2,1)} %get-tuple-element.6, f32[96]{0:T(128)S(1)} %add_rsqrt_fusion), kind=kOutput, calls=%fused_computation.2 | convolution fusion | flops 1590042624 | bytes 18628992 | tf_op jit(solution)/shard_map/dot_general | solution.py:84
  200.6 0.0 reduce-scatter.2.cloned.1.call-update
  200.6 19.7 %reduce-scatter.2.cloned.1.call-done = bf16[24,1792]{1,0:T(8,128)(2,1)} async-done(((bf16[96,1792]{1,0:T(8,128)(2,1)}), bf16[24,1792]{1,0:T(8,128)(2,1)}) %reduce-scatter.2.cloned.1.call-update) | async-done | bytes 86032 | tf_op jit(solution)/shard_map/reduce_scatter | solution.py:83
  220.4 1.5 add_convert_fusion
  (5 shorter events, 0.1 us)
Async XLA Ops:
  6.5 4.6 %copy-start.5 = (bf16[6,512,512]{2,1,0:T(8,128)(2,1)S(1)}, bf16[6,512,512]{2,1,0:T(8,128)(2,1)}, u32[]{:S(2)}) copy-start(bf16[6,512,512]{2,1,0:T(8,128)(2,1)} %param.11) | copy-start | bytes 9437188
  6.5 4.2 %copy-start.4 = (s32[6]{0:T(128)S(1)}, s32[6]{0:T(128)}, u32[]{:S(2)}) copy-start(s32[6]{0:T(128)} %param.13) | copy-start | bytes 76
  38.4 15.1 %all-to-all-start = ((bf16[24,4,4096]{2,0,1:T(8,128)(2,1)}), bf16[24,4,4096]{2,0,1:T(8,128)(2,1)S(1)}, u32[]{:S(2)}, u32[]{:S(2)}) async-start(bf16[24,4,4096]{2,0,1:T(8,128)(2,1)} %copy.12), calls=%async_computation | async-start | bytes 1572864 | tf_op jit(solution)/shard_map/all_to_all | solution.py:59
  41.9 53.6 %all-reduce.4.cloned.1.call-start = ((), (), s32[]{:S(2)}) async-start(), calls=%async_computation.2 | async-start | bytes 1376256 | tf_op jit(solution)/shard_map/psum | solution.py:68
  53.5 7.6 %copy-start.2 = (bf16[24,1792]{1,0:T(8,128)(2,1)S(1)}, bf16[24,1792]{1,0:T(8,128)(2,1)}, u32[]{:S(2)}) copy-start(bf16[24,1792]{1,0:T(8,128)(2,1)} %param.14) | copy-start | bytes 258052
  53.5 8.6 %copy-start.3 = (bf16[1792]{0:T(1024)(128)(2,1)S(1)}, bf16[1792]{0:T(1024)(128)(2,1)}, u32[]{:S(2)}) copy-start(bf16[1792]{0:T(1024)(128)(2,1)} %param.16) | copy-start | bytes 10756
  61.2 0.8 copy-start.1
  62.1 128.5 %all-reduce.6.cloned.1.call-start = ((), (), s32[]{:S(2)}) async-start(), calls=%async_computation.4 | async-start | bytes 3538944 | tf_op jit(solution)/shard_map/psum | solution.py:76
  95.5 9.6 %copy-start = (f32[96,1792]{1,0:T(8,128)S(1)}, f32[96,1792]{1,0:T(8,128)}, u32[]{:S(2)}) copy-start(f32[96,1792]{1,0:T(8,128)} %all-reduce.4.cloned.1.call-done) | copy-start | bytes 2064388
  114.5 105.8 %reduce-scatter.2.cloned.1.call-start = ((), (), s32[]{:S(2)}) async-start(), calls=%async_computation.3 | async-start | bytes 430080 | tf_op jit(solution)/shard_map/reduce_scatter | solution.py:83
Sparse Core Ops, SparseCore 0:
  62.2 33.2 all-reduce.3
  114.7 75.9 all-reduce.5
  200.7 19.5 reduce-scatter.1
where the time goes:
time: 229 us; the launch traced here: 228 us
  waiting for transfers between devices  128 us (56%)
  matrix products  40.3 us (18%)
  blocking collectives  36.4 us (16%)
  between operations  13.2 us (6%)
  starting transfers between devices  3.62 us (2%)
  local copies, waits for them, and re-layouts  3.51 us (2%)
  other arithmetic  2.92 us (1%)
    psum x1, waiting for transfers between devices, finish_rows(): lax.psum(up_part.astype(jnp.bfloat16), 'tp').astype(jnp.float32)  63.7 us
    psum x1, waiting for transfers between devices, finish_rows(): post_attn = lax.psum(summand, 'pool')  33.4 us
    all_gather x1, blocking collectives, finish_rows(): columns = lax.all_gather(attended, 'tp', axis=0, tiled=True)  24.2 us
    reduce_scatter x1, waiting for transfers between devices, finish_rows(): lax.psum_scatter(jnp.dot(hidden, down_weight, preferred_element_type=jnp....  19.7 us
    psum x1, blocking collectives, finish_rows(): lax.psum(squares.astype(jnp.bfloat16), 'tp').astype(jnp.float32)  12.2 us
    all_to_all x1, waiting for transfers between devices, finish_rows(): lax.all_to_all(columns, 'pool', split_axis=1, concat_axis=0, tiled=True)  11.6 us
    dot_general x1, matrix products, finish_rows(): jnp.dot(hidden, down_weight, preferred_element_type=jnp.float32)  9.94 us
    dot_general x1, matrix products, finish_rows(): up_part = jnp.dot(scaled, up_weight, preferred_element_type=jnp.float32)  9.61 us
  transfers between devices with their start and end apart: 4, of which 4 were waited for; matrix products, arithmetic and copies ran while one was open for 0% of the time, Pallas kernels for 0%

commit v1 on v0

--- a/solution.py
+++ b/solution.py
@@ -55,7 +55,16 @@
     shard_count = lax.axis_size("tp")
     pool_at = lax.axis_index("pool")
     attended = attend(queries, cached_entries, new_entry, lengths)
-    columns = lax.all_gather(attended, "tp", axis=0, tiled=True)
+    ways = lax.axis_size("tp")
+    up = [(d, (d + 1) % ways) for d in range(ways)]
+    down = [(d, (d - 1) % ways) for d in range(ways)]
+    earlier, later = ([attended], [attended])
+    for _ in range(ways // 2):
+        earlier.append(lax.ppermute(earlier[-1], "tp", up))
+    for _ in range((ways - 1) // 2):
+        later.append(lax.ppermute(later[-1], "tp", down))
+    line = jnp.concatenate([*earlier[::-1], *later[1:]], axis=0)
+    columns = jnp.roll(line, (lax.axis_index("tp") - ways // 2) * attended.shape[0], axis=0)
     spread = lax.all_to_all(columns, "pool", split_axis=1, concat_axis=0, tiled=True)
     block_rows = shard_count * queries.shape[0]
     resid_flat = resid_rows.reshape(block_rows, resid_rows.shape[2]).astype(jnp.float32)

time: 229 us -> 228 us (level)
  blocking collectives: 36.4 us -> 11.9 us
  waiting for transfers between devices: 128 us -> 145 us
  starting transfers between devices: 3.62 us -> 8.79 us
    all_gather x1 -> x0, blocking collectives: 24.2 us -> none  [finish_rows(): columns = lax.all_gather(attended, 'tp', axis=0, tiled=True)]
    ppermute x0 -> x3, waiting for transfers between devices: none -> 17.5 us  [the longest x2 13.1 us: finish_rows(): earlier.append(lax.ppermute(earlier[-1], 'tp', up))]
    ppermute x0 -> x3, starting transfers between devices: none -> 5.17 us  [the longest x2 3.08 us: finish_rows(): earlier.append(lax.ppermute(earlier[-1], 'tp', up))]
    concatenate x0 -> x1, local copies, waits for them, and re-layouts: none -> 3.47 us  [finish_rows(): jnp.roll(line, (lax.axis_index('tp') - ways // 2) * attended.shape[0], ax...]
  transfers between devices with their start and end apart: 4 -> 7, of which waited for: 4 -> 7; matrix products, arithmetic and copies ran while one was open for 0% -> 0% of each run, Pallas kernels for 0% -> 0%
where the time goes in v1:
time: 228 us
  waiting for transfers between devices  145 us (64%)
  matrix products  40.4 us (18%)
  between operations  13.2 us (6%)
  blocking collectives  11.9 us (5%)
  starting transfers between devices  8.79 us (4%)
  local copies, waits for them, and re-layouts  5.6 us (2%)
  other arithmetic  2.92 us (1%)
    psum x1, waiting for transfers between devices, finish_rows(): lax.psum(up_part.astype(jnp.bfloat16), 'tp').astype(jnp.float32)  64 us
    psum x1, waiting for transfers between devices, finish_rows(): post_attn = lax.psum(summand, 'pool')  32.5 us
    reduce_scatter x1, waiting for transfers between devices, finish_rows(): lax.psum_scatter(jnp.dot(hidden, down_weight, preferred_element_type=jnp....  19.7 us
    ppermute x2, waiting for transfers between devices, finish_rows(): earlier.append(lax.ppermute(earlier[-1], 'tp', up))  13.1 us
    psum x1, blocking collectives, finish_rows(): lax.psum(squares.astype(jnp.bfloat16), 'tp').astype(jnp.float32)  11.9 us
    all_to_all x1, waiting for transfers between devices, finish_rows(): lax.all_to_all(columns, 'pool', split_axis=1, concat_axis=0, tiled=True)  11.6 us
    dot_general x1, matrix products, finish_rows(): jnp.dot(hidden, down_weight, preferred_element_type=jnp.float32)  9.94 us
    dot_general x1, matrix products, finish_rows(): up_part = jnp.dot(scaled, up_weight, preferred_element_type=jnp.float32)  9.62 us
  transfers between devices with their start and end apart: 7, of which 7 were waited for; matrix products, arithmetic and copies ran while one was open for 0% of the time, Pallas kernels for 0%

profile of v1, /device:TPU:0, one launch (start us, length us, event | category | flops | bytes accessed | tf_op | source)
XLA Modules:
  0.0 228.1 jit_solution(1850640797119709984)
XLA Ops:
  6.5 0.0 copy-start.5
  6.5 0.0 copy-start.4
  6.5 0.9 slice_convert_fusion
  7.4 1.2 fusion.26
  8.6 2.1 fusion.39
  10.8 0.0 copy-done.4
  10.8 0.3 fusion.21
  11.1 0.0 copy-done.5
  11.1 0.5 fusion.16
  11.6 0.1 copy.17
  11.7 3.1 %collective-permute-start = (bf16[6,16384]{1,0:T(8,128)(2,1)S(1)}, bf16[6,16384]{1,0:T(8,128)(2,1)S(1)}, u32[]{:S(2)}, u32[]{:S(2)}) collective-permute-start(bf16[6,16384]{1,0:T(8,128)(2,1)S(1)} %bitcast.45), channel_id=1, source_target_pairs={{0,1},{1,2},{2,3},{3,0},{4,5},{5,6},{6,7},{7,4},{8,9},{9,10},{10,1... | collective-permute-start | bytes 589832 | tf_op jit(solution)/shard_map/ppermute | solution.py:63
  14.8 2.1 collective-permute-start.2
  16.9 7.1 %collective-permute-done = bf16[6,16384]{1,0:T(8,128)(2,1)S(1)} collective-permute-done((bf16[6,16384]{1,0:T(8,128)(2,1)S(1)}, bf16[6,16384]{1,0:T(8,128)(2,1)S(1)}, u32[]{:S(2)}, u32[]{:S(2)}) %collective-permute-start) | collective-permute-done | bytes 196640 | tf_op jit(solution)/shard_map/ppermute | solution.py:63
  24.0 0.0 collective-permute-start.1
  24.0 4.4 %collective-permute-done.2 = bf16[6,16384]{1,0:T(8,128)(2,1)S(1)} collective-permute-done((bf16[6,16384]{1,0:T(8,128)(2,1)S(1)}, bf16[6,16384]{1,0:T(8,128)(2,1)S(1)}, u32[]{:S(2)}, u32[]{:S(2)}) %collective-permute-start.2) | collective-permute-done | bytes 196640 | tf_op jit(solution)/shard_map/ppermute | solution.py:65
  28.4 6.0 %collective-permute-done.1 = bf16[6,16384]{1,0:T(8,128)(2,1)S(1)} collective-permute-done((bf16[6,16384]{1,0:T(8,128)(2,1)S(1)}, bf16[6,16384]{1,0:T(8,128)(2,1)S(1)}, u32[]{:S(2)}, u32[]{:S(2)}) %collective-permute-start.1) | collective-permute-done | bytes 196640 | tf_op jit(solution)/shard_map/ppermute | solution.py:63
  34.4 3.5 %concatenate.6 = bf16[48,16384]{1,0:T(8,128)(2,1)S(1)} concatenate(bf16[6,16384]{1,0:T(8,128)(2,1)S(1)} %collective-permute-done.1, bf16[6,16384]{1,0:T(8,128)(2,1)S(1)} %collective-permute-done, bf16[6,16384]{1,0:T(8,128)(2,1)S(1)} %bitcast.47, bf16[6,16384]{1,0:T(8,128)(2,1)S(1)} %collective-permute-done.2, bf16[6,16384]{1,0:T(8,128)(2,1)S(1)} %collective-permute-done.1, ...), dimensions={0} | concatenate | bytes 3145728 | tf_op jit(solution)/shard_map/jit(_roll_dynamic)/concatenate | solution.py:67
  37.8 0.2 constant_dynamic-slice_fusion
  38.1 0.9 copy.48
  39.0 3.5 %all-to-all-start = ((bf16[24,4,4096]{2,0,1:T(8,128)(2,1)}), bf16[24,4,4096]{2,0,1:T(8,128)(2,1)S(1)}, u32[]{:S(2)}, u32[]{:S(2)}) async-start(bf16[24,4,4096]{2,0,1:T(8,128)(2,1)} %bitcast.42), calls=%async_computation | async-start | bytes 1572864 | tf_op jit(solution)/shard_map/all_to_all | solution.py:68
  42.5 0.0 all-reduce.4.cloned.1.call-start
  42.6 11.6 %all-to-all-done = bf16[24,4,4096]{2,0,1:T(8,128)(2,1)S(1)} async-done(((bf16[24,4,4096]{2,0,1:T(8,128)(2,1)}), bf16[24,4,4096]{2,0,1:T(8,128)(2,1)S(1)}, u32[]{:S(2)}, u32[]{:S(2)}) %all-to-all-start) | async-done | bytes 786464 | tf_op jit(solution)/shard_map/all_to_all | solution.py:68
  54.1 0.0 copy-start.2
  54.1 0.0 copy-start.3
  54.1 7.7 %fusion.40 = f32[96,1792]{1,0:T(8,128)S(1)} fusion(bf16[96,4096]{1,0:T(8,128)(2,1)S(1)} %bitcast.43, bf16[4096,1792]{1,0:T(8,128)(2,1)} %param.15), kind=kOutput, calls=%fused_computation.48 | convolution fusion | flops 1409286144 | bytes 16154624 | tf_op jit(solution)/shard_map/dot_general | solution.py:72
  61.8 0.0 copy-done.2
  61.8 0.0 copy-start.1
  61.8 0.8 copy-done.1
  62.7 0.0 all-reduce.4.cloned.1.call-update
  62.7 0.0 all-reduce.6.cloned.1.call-start
  62.8 0.0 copy-done.3
  62.8 32.5 %all-reduce.4.cloned.1.call-done = f32[96,1792]{1,0:T(8,128)} async-done(((f32[96,1792]{1,0:T(8,128)}), f32[96,1792]{1,0:T(8,128)}) %all-reduce.4.cloned.1.call-update) | async-done | bytes 688144 | tf_op jit(solution)/shard_map/psum | solution.py:77
  95.2 0.0 copy-start
  95.2 9.6 %convolution_convert_fusion = bf16[96,4608]{1,0:T(8,128)(2,1)} fusion(bf16[1792,4608]{1,0:T(8,128)(2,1)} %param.18, f32[96,1792]{1,0:T(8,128)} %all-reduce.4.cloned.1.call-done, f32[1792]{0:T(1024)S(1)} %convert_element_type.65), kind=kOutput, calls=%fused_computation | convolution fusion | flops 1586233344 | bytes 18095104 | tf_op jit(solution)/shard_map/dot_general | solution.py:82
  104.9 0.0 copy-done
  104.9 9.3 %convolution_convert_fusion.1 = bf16[96,4608]{1,0:T(8,128)(2,1)} fusion(bf16[1792,4608]{1,0:T(8,128)(2,1)} %param.17, f32[96,1792]{1,0:T(8,128)S(1)} %copy-done, f32[1792]{0:T(1024)S(1)} %convert_element_type.65), kind=kOutput, calls=%fused_computation.1 | convolution fusion | flops 1586233344 | bytes 18095104 | tf_op jit(solution)/shard_map/dot_general | solution.py:81
  114.2 0.0 all-reduce.6.cloned.1.call-update
  114.2 0.0 reduce-scatter.2.cloned.1.call-start
  114.3 0.1 multiply_reduce_fusion
  114.4 11.9 %psum.30 = bf16[96]{0:T(256)(128)(2,1)S(1)} all-reduce(bf16[96]{0:T(256)(128)(2,1)S(1)} %multiply_reduce_fusion), channel_id=1, replica_groups=mesh['groups'=2,'pool'=4,'tp'=4] {'tp'}, use_global_device_ids=true, to_apply=%region_5.6 | all-reduce | flops 96 | bytes 384 | tf_op jit(solution)/shard_map/psum | solution.py:86
  126.4 64.0 %all-reduce.6.cloned.1.call-done = (bf16[96,4608]{1,0:T(8,128)(2,1)}, bf16[96,4608]{1,0:T(8,128)(2,1)}) async-done(((bf16[96,4608]{1,0:T(8,128)(2,1)}, bf16[96,4608]{1,0:T(8,128)(2,1)}), (bf16[96,4608]{1,0:T(8,128)(2,1)}, bf16[96,4608]{1,0:T(8,128)(2,1)})) %all-reduce.6.cloned.1.call-update) | async-done | bytes 1769488 | tf_op jit(solution)/shard_map/psum | solution.py:85
  190.3 9.9 %convolution_convert_fusion.2 = bf16[96,1792]{1,0:T(8,128)(2,1)} fusion(bf16[4608,1792]{1,0:T(8,128)(2,1)} %param.19, bf16[96,4608]{1,0:T(8,128)(2,1)} %get-tuple-element.5, bf16[96,4608]{1,0:T(8,128)(2,1)} %get-tuple-element.6, f32[96]{0:T(128)S(1)} %add_rsqrt_fusion), kind=kOutput, calls=%fused_computation.2 | convolution fusion | flops 1590042624 | bytes 18628992 | tf_op jit(solution)/shard_map/dot_general | solution.py:93
  200.3 0.0 reduce-scatter.2.cloned.1.call-update
  200.3 19.7 %reduce-scatter.2.cloned.1.call-done = bf16[24,1792]{1,0:T(8,128)(2,1)} async-done(((bf16[96,1792]{1,0:T(8,128)(2,1)}), bf16[24,1792]{1,0:T(8,128)(2,1)}) %reduce-scatter.2.cloned.1.call-update) | async-done | bytes 86032 | tf_op jit(solution)/shard_map/reduce_scatter | solution.py:92
  220.1 1.5 add_convert_fusion
  (5 shorter events, 0.1 us)
Async XLA Ops:
  6.5 4.6 %copy-start.5 = (bf16[6,512,512]{2,1,0:T(8,128)(2,1)S(1)}, bf16[6,512,512]{2,1,0:T(8,128)(2,1)}, u32[]{:S(2)}) copy-start(bf16[6,512,512]{2,1,0:T(8,128)(2,1)} %param.11) | copy-start | bytes 9437188
  6.5 4.2 %copy-start.4 = (s32[6]{0:T(128)S(1)}, s32[6]{0:T(128)}, u32[]{:S(2)}) copy-start(s32[6]{0:T(128)} %param.13) | copy-start | bytes 76
  11.7 12.3 %collective-permute-start = (bf16[6,16384]{1,0:T(8,128)(2,1)S(1)}, bf16[6,16384]{1,0:T(8,128)(2,1)S(1)}, u32[]{:S(2)}, u32[]{:S(2)}) collective-permute-start(bf16[6,16384]{1,0:T(8,128)(2,1)S(1)} %bitcast.45), channel_id=1, source_target_pairs={{0,1},{1,2},{2,3},{3,0},{4,5},{5,6},{6,7},{7,4},{8,9},{9,10},{10,1... | collective-permute-start | bytes 589832 | tf_op jit(solution)/shard_map/ppermute | solution.py:63
  14.8 13.6 %collective-permute-start.2 = (bf16[6,16384]{1,0:T(8,128)(2,1)S(1)}, bf16[6,16384]{1,0:T(8,128)(2,1)S(1)}, u32[]{:S(2)}, u32[]{:S(2)}) collective-permute-start(bf16[6,16384]{1,0:T(8,128)(2,1)S(1)} %bitcast.46), channel_id=1, source_target_pairs={{0,3},{1,0},{2,1},{3,2},{4,7},{5,4},{6,5},{7,6},{8,11},{9,8},{10,9... | collective-permute-start | bytes 589832 | tf_op jit(solution)/shard_map/ppermute | solution.py:65
  24.0 10.4 %collective-permute-start.1 = (bf16[6,16384]{1,0:T(8,128)(2,1)S(1)}, bf16[6,16384]{1,0:T(8,128)(2,1)S(1)}, u32[]{:S(2)}, u32[]{:S(2)}) collective-permute-start(bf16[6,16384]{1,0:T(8,128)(2,1)S(1)} %collective-permute-done), channel_id=1, source_target_pairs={{0,1},{1,2},{2,3},{3,0},{4,5},{5,6},{6,7},{7,4},{8,9},{9,10},{10,1... | collective-permute-start | bytes 589832 | tf_op jit(solution)/shard_map/ppermute | solution.py:63
  39.0 15.1 %all-to-all-start = ((bf16[24,4,4096]{2,0,1:T(8,128)(2,1)}), bf16[24,4,4096]{2,0,1:T(8,128)(2,1)S(1)}, u32[]{:S(2)}, u32[]{:S(2)}) async-start(bf16[24,4,4096]{2,0,1:T(8,128)(2,1)} %bitcast.42), calls=%async_computation | async-start | bytes 1572864 | tf_op jit(solution)/shard_map/all_to_all | solution.py:68
  42.5 52.7 %all-reduce.4.cloned.1.call-start = ((), (), s32[]{:S(2)}) async-start(), calls=%async_computation.2 | async-start | bytes 1376256 | tf_op jit(solution)/shard_map/psum | solution.py:77
  54.1 7.7 %copy-start.2 = (bf16[24,1792]{1,0:T(8,128)(2,1)S(1)}, bf16[24,1792]{1,0:T(8,128)(2,1)}, u32[]{:S(2)}) copy-start(bf16[24,1792]{1,0:T(8,128)(2,1)} %param.14) | copy-start | bytes 258052
  54.1 8.6 %copy-start.3 = (bf16[1792]{0:T(1024)(128)(2,1)S(1)}, bf16[1792]{0:T(1024)(128)(2,1)}, u32[]{:S(2)}) copy-start(bf16[1792]{0:T(1024)(128)(2,1)} %param.16) | copy-start | bytes 10756
  61.8 0.9 copy-start.1
  62.7 127.6 %all-reduce.6.cloned.1.call-start = ((), (), s32[]{:S(2)}) async-start(), calls=%async_computation.4 | async-start | bytes 3538944 | tf_op jit(solution)/shard_map/psum | solution.py:85
  95.2 9.6 %copy-start = (f32[96,1792]{1,0:T(8,128)S(1)}, f32[96,1792]{1,0:T(8,128)}, u32[]{:S(2)}) copy-start(f32[96,1792]{1,0:T(8,128)} %all-reduce.4.cloned.1.call-done) | copy-start | bytes 2064388
  114.2 105.8 %reduce-scatter.2.cloned.1.call-start = ((), (), s32[]{:S(2)}) async-start(), calls=%async_computation.3 | async-start | bytes 430080 | tf_op jit(solution)/shard_map/reduce_scatter | solution.py:92
Sparse Core Ops, SparseCore 0:
  62.8 32.3 all-reduce.3
  114.4 75.9 all-reduce.5
  200.4 19.5 reduce-scatter.1
